TPU v7x, 512 devices: a whole 4x4x16 slice. The times are simulated.
512 devices in a mesh: rows: 64 (over x, z_lo, core), cols: 8 (over y, z_hi).
Axes of the slice: x: 4, y: 4, z: 16 (z_hi: 2, z_lo: 8; z = z_hi * 8 + z_lo), core: 2. Of those that a mesh axis runs over, the one named last changes fastest.
Arguments:
- features: bfloat16 [786432, 256], P(('rows', 'cols')), may hold values from -6 to 6
- adj_values: bfloat16 [6144, 3, 128, 128], P(('rows', 'cols')), may hold values from -0.3125 to 0.3125
- adj_offset: int32 [6144, 3], P(('rows', 'cols')), may hold values from -2 to 2, as said below
- adj_count: int32 [6144], P(('rows', 'cols')), may hold values from 1 to 3, as said below
- weight: bfloat16 [256, 256], replicated, may hold values from -0.375 to 0.375
- bias_vector: float32 [256], replicated, may hold values from -4 to 4
- cotangent: bfloat16 [786432, 256], P(('rows', 'cols')), may hold values from -6 to 6
Outputs:
- activated: bfloat16 [786432, 256], P(('rows', 'cols'))
- grad_features: bfloat16 [786432, 256], P(('rows', 'cols'))
- grad_weight: float32 [256, 256], replicated
- grad_bias: float32 [256], replicated
Inputs may be any that keep to these rules, and one draw needn't show every extreme that they name: Slot 0 of every row block has offset 0; the offsets of one row block are distinct, and for row block i every i + adj_offset[i, s] lies in 0 to 6143. Row block i uses its slots 0 to adj_count[i] - 1; the values and offsets of its other slots are ignored. In every draw all row blocks of one device, drawn from the seed, use all 3 slots.
All inputs are finite; a program needn't handle non-finite values.
Results may differ from a plain program's by a relative error of at most 0.0075.
Values may be sent and summed in bfloat16 or wider, within the bound.
A program may use at most 64 MiB of HBM per device.

v0:
```python
import math
import jax
import jax.numpy as jnp
from jax import lax
from jax.sharding import PartitionSpec as P

BAND = 2


def shifted(value, axis, steps):
    count = lax.axis_size(axis)
    pairs = [(source, (source + steps) % count) for source in range(count)]
    return lax.ppermute(value, axis, pairs)


def from_behind(value, axis, steps):
    count = lax.axis_size(axis)
    initial, last = (max(0, -steps), min(count, count - steps))
    return lax.ppermute(value, axis, [(source, source + steps) for source in range(initial, last)])


def fetch_lower(rim_piece):
    narrow_step = shifted(rim_piece, "cols", 1)
    wide_step = from_behind(narrow_step, "rows", 1)
    return jnp.where(lax.axis_index("cols") == 0, wide_step, narrow_step)


def fetch_upper(rim_piece):
    narrow_step = shifted(rim_piece, "cols", -1)
    wide_step = from_behind(narrow_step, "rows", -1)
    return jnp.where(lax.axis_index("cols") == lax.axis_size("cols") - 1, wide_step, narrow_step)


def spill_lower(rim_piece):
    narrow_step = shifted(rim_piece, "cols", 1)
    wide_step = from_behind(narrow_step, "rows", 1)
    return jnp.where(lax.axis_index("cols") == 0, wide_step, narrow_step)


def spill_upper(rim_piece):
    narrow_step = shifted(rim_piece, "cols", -1)
    wide_step = from_behind(narrow_step, "rows", -1)
    return jnp.where(lax.axis_index("cols") == lax.axis_size("cols") - 1, wide_step, narrow_step)


def on_device(features, adj_values, adj_offset, adj_count, weight, bias_vector, cotangent):
    blocks = adj_offset.shape[0]
    slot_total = adj_offset.shape[1]
    block_rows = adj_values.shape[2]
    feat_width = features.shape[1]
    band_reach = BAND
    span_blocks = blocks + 2 * band_reach
    rim_rows = band_reach * block_rows
    slot_index = lax.broadcasted_iota(jnp.int32, (blocks, slot_total), 1)
    block_index = lax.broadcasted_iota(jnp.int32, (blocks, slot_total), 0)
    active = slot_index < adj_count[:, None]
    target = block_index + band_reach + adj_offset
    from_below = fetch_lower(features[features.shape[0] - rim_rows :])
    from_above = fetch_upper(features[:rim_rows])
    extended = jnp.concatenate([from_below, features, from_above], 0)
    window = extended.reshape(span_blocks, block_rows, feat_width)
    picked = window[target]
    picked = jnp.where(active[:, :, None, None], picked, jnp.zeros_like(picked))
    summed = jnp.einsum("bsac,bscf->baf", adj_values, picked, preferred_element_type=jnp.float32)
    aggregated = summed.reshape(-1, feat_width).astype(jnp.bfloat16)
    preact = jnp.dot(aggregated, weight, preferred_element_type=jnp.float32) + bias_vector
    activated = jax.nn.silu(preact).astype(jnp.bfloat16)
    sigmoid_pre = jax.nn.sigmoid(preact)
    grad_pre = (
        cotangent.astype(jnp.float32) * sigmoid_pre * (1.0 + preact * (1.0 - sigmoid_pre))
    ).astype(jnp.bfloat16)
    partial_weight = lax.dot_general(
        aggregated, grad_pre, (((0,), (0,)), ((), ())), preferred_element_type=jnp.float32
    )
    partial_bias = jnp.sum(grad_pre.astype(jnp.float32), axis=0)
    total_weight, total_bias = lax.psum((partial_weight, partial_bias), ("rows", "cols"))
    nodes_total = features.shape[0] * lax.axis_size("rows") * lax.axis_size("cols")
    norm_scale = 1.0 / math.sqrt(nodes_total)
    grad_weight = total_weight * norm_scale
    grad_bias = total_bias * norm_scale
    upstream = lax.dot_general(
        grad_pre, weight, (((1,), (1,)), ((), ())), preferred_element_type=jnp.float32
    ).astype(jnp.bfloat16)
    slot_terms = jnp.einsum(
        "bsac,baf->bscf",
        adj_values,
        upstream.reshape(blocks, block_rows, feat_width),
        preferred_element_type=jnp.float32,
    )
    slot_terms = jnp.where(active[:, :, None, None], slot_terms, jnp.zeros_like(slot_terms))
    empty = jnp.zeros((span_blocks, block_rows, feat_width), jnp.float32)
    spread = empty.at[target.reshape(-1)].add(slot_terms.reshape(-1, block_rows, feat_width))
    lower_part = spread[:band_reach]
    middle = spread[band_reach : band_reach + blocks]
    upper_part = spread[band_reach + blocks :]
    from_above_dev = spill_upper(lower_part)
    from_below_dev = spill_lower(upper_part)
    combined = middle.at[:band_reach].add(from_below_dev)
    combined = combined.at[blocks - band_reach :].add(from_above_dev)
    grad_features = combined.reshape(-1, feat_width).astype(jnp.bfloat16)
    return (activated, grad_features, grad_weight, grad_bias)


def solution(mesh):
    return jax.shard_map(
        on_device,
        mesh=mesh,
        in_specs=(
            P(("rows", "cols"), None),
            P(("rows", "cols"), None, None, None),
            P(("rows", "cols"), None),
            P(("rows", "cols")),
            P(),
            P(),
            P(("rows", "cols"), None),
        ),
        out_specs=(P(("rows", "cols"), None), P(("rows", "cols"), None), P(), P()),
        check_vma=False,
    )
```

profile of v0, /device:TPU:4, one launch (start us, length us, event | category | flops | bytes accessed | tf_op | source)
XLA Modules:
  0.0 578.7 jit_solution(4762388384572714263)
XLA Ops:
  8.4 15.7 %collective-permute-start = (bf16[256,256]{1,0:T(8,128)(2,1)S(1)}, bf16[256,256]{1,0:T(8,128)(2,1)S(1)}, u32[]{:S(2)}, u32[]{:S(2)}) collective-permute-start(bf16[256,256]{1,0:T(8,128)(2,1)S(1)} %get-tuple-element.35), channel_id=1, source_target_pairs={{0,1},{1,2},{2,3},{3,4},{4,5},{5,6},{6,7},{7,0},{8,9},{9,10},{10,1... | collective-permute-start | bytes 393224 | tf_op jit(solution)/shard_map/ppermute | solution.py:13
  24.1 4.4 collective-permute-start.2
  30.3 1.9 collective-permute-start.1
  32.4 19.6 %collective-permute-done.2 = bf16[256,256]{1,0:T(8,128)(2,1)S(1)} collective-permute-done((bf16[256,256]{1,0:T(8,128)(2,1)S(1)}, bf16[256,256]{1,0:T(8,128)(2,1)S(1)}, u32[]{:S(2)}, u32[]{:S(2)}) %collective-permute-start.2) | collective-permute-done | bytes 131104 | tf_op jit(solution)/shard_map/ppermute | solution.py:13
  52.0 1.9 collective-permute-start.3
  54.0 2.5 collective-permute-done.3
  56.6 2.3 gather_fusion
  58.9 2.4 bitcast_convert_fusion
  61.3 1.8 convert_reduce_fusion
  64.4 3.1 broadcast_select_fusion
  67.5 6.1 %copy.17 = f32[36,128,256]{2,1,0:T(8,128)} copy(f32[36,128,256]{1,2,0:T(8,128)} %bitcast.28) | data formatting | bytes 9437184 | tf_op jit(solution)/shard_map/reshape | solution.py:92
  73.9 8.9 %scatter_fusion = f32[16,128,256]{2,1,0:T(8,128)S(1)} fusion(f32[16,128,256]{2,1,0:T(8,128)S(1)} %broadcast_in_dim.36, s32[36]{0:T(128)S(1)} %fusion.8, f32[36,128,256]{2,1,0:T(8,128)} %copy.17), kind=kCustom, calls=%fused_computation.1 | custom fusion | flops 1179648 | bytes 14155920 | tf_op jit(solution)/shard_map/scatter-add | solution.py:92
  83.6 8.7 %collective-permute-start.4 = (f32[2,128,256]{2,1,0:T(8,128)}, f32[2,128,256]{2,1,0:T(8,128)}, u32[]{:S(2)}, u32[]{:S(2)}) collective-permute-start(f32[2,128,256]{2,1,0:T(8,128)} %get-tuple-element.33), channel_id=1, source_target_pairs={{0,1},{1,2},{2,3},{3,4},{4,5},{5,6},{6,7},{7,0},{8,9},{9,10},{10,1... | collective-permute-start | bytes 786440 | tf_op jit(solution)/shard_map/ppermute | solution.py:13
  92.3 7.9 %collective-permute-start.6 = (f32[2,128,256]{2,1,0:T(8,128)}, f32[2,128,256]{2,1,0:T(8,128)S(1)}, u32[]{:S(2)}, u32[]{:S(2)}) collective-permute-start(f32[2,128,256]{2,1,0:T(8,128)} %get-tuple-element.32), channel_id=1, source_target_pairs={{0,7},{1,0},{2,1},{3,2},{4,3},{5,4},{6,5},{7,6},{8,15},{9,8},{10,9... | collective-permute-start | bytes 786440 | tf_op jit(solution)/shard_map/ppermute | solution.py:13
  100.2 2.5 fusion.12
  102.8 108.2 %psum.15 = f32[256]{0:T(256)S(1)} all-reduce(f32[256]{0:T(256)S(1)} %get-tuple-element.28), channel_id=1, replica_groups=mesh['rows'=64,'cols'=8] {'rows','cols'}, use_global_device_ids=true, to_apply=%region_3.4 | all-reduce | flops 256 | bytes 2048 | tf_op jit(solution)/shard_map/psum | solution.py:76
  210.9 1.9 collective-permute-start.5
  213.4 1.3 slice.73
  214.7 11.1 %collective-permute-start.7 = (f32[2,128,256]{2,1,0:T(8,128)S(1)}, f32[2,128,256]{2,1,0:T(8,128)}, u32[]{:S(2)}, u32[]{:S(2)}) collective-permute-start(f32[2,128,256]{2,1,0:T(8,128)S(1)} %collective-permute-done.6), channel_id=1, source_target_pairs={{8,0},{16,8},{24,16},{32,24},{40,32},{48,40},{56,48},{64,56},{72,6... | collective-permute-start | bytes 786440 | tf_op jit(solution)/shard_map/ppermute | solution.py:19
  225.9 338.5 %all-reduce.2.cloned.1.call-done = f32[256,256]{1,0:T(8,128)} async-done(((f32[256,256]{1,0:T(8,128)}), f32[256,256]{1,0:T(8,128)}) %all-reduce.2.cloned.1.call-update) | async-done | bytes 262160 | tf_op jit(solution)/shard_map/psum | solution.py:76
  564.3 1.7 broadcast_multiply_fusion
  566.0 1.7 fusion.7
  567.7 1.7 fusion.6
  569.5 2.4 convert_element_type.37
  (39 shorter events, 6.2 us)
Async XLA Ops:
  7.2 51.7 %copy-start = (bf16[12,3,128,128]{3,2,1,0:T(8,128)(2,1)S(1)}, bf16[12,3,128,128]{3,2,1,0:T(8,128)(2,1)}, u32[]{:S(2)}) copy-start(bf16[12,3,128,128]{3,2,1,0:T(8,128)(2,1)} %param.12) | copy-start | bytes 3538948
  7.2 49.3 %copy-start.1 = (bf16[1536,256]{1,0:T(8,128)(2,1)S(1)}, bf16[1536,256]{1,0:T(8,128)(2,1)}, u32[]{:S(2)}) copy-start(bf16[1536,256]{1,0:T(8,128)(2,1)} %param.11) | copy-start | bytes 2359300
  7.2 557.1 %all-reduce.2.cloned.1.call-start = ((), (), s32[]{:S(2)}) async-start(), calls=%async_computation | async-start | bytes 524288 | tf_op jit(solution)/shard_map/psum | solution.py:76
  8.4 22.0 %collective-permute-start = (bf16[256,256]{1,0:T(8,128)(2,1)S(1)}, bf16[256,256]{1,0:T(8,128)(2,1)S(1)}, u32[]{:S(2)}, u32[]{:S(2)}) collective-permute-start(bf16[256,256]{1,0:T(8,128)(2,1)S(1)} %get-tuple-element.35), channel_id=1, source_target_pairs={{0,1},{1,2},{2,3},{3,4},{4,5},{5,6},{6,7},{7,0},{8,9},{9,10},{10,1... | collective-permute-start | bytes 393224 | tf_op jit(solution)/shard_map/ppermute | solution.py:13
  24.1 28.0 %collective-permute-start.2 = (bf16[256,256]{1,0:T(8,128)(2,1)S(1)}, bf16[256,256]{1,0:T(8,128)(2,1)S(1)}, u32[]{:S(2)}, u32[]{:S(2)}) collective-permute-start(bf16[256,256]{1,0:T(8,128)(2,1)S(1)} %get-tuple-element.36), channel_id=1, source_target_pairs={{0,7},{1,0},{2,1},{3,2},{4,3},{5,4},{6,5},{7,6},{8,15},{9,8},{10,9... | collective-permute-start | bytes 393224 | tf_op jit(solution)/shard_map/ppermute | solution.py:13
  30.3 23.7 %collective-permute-start.1 = (bf16[256,256]{1,0:T(8,128)(2,1)S(1)}, bf16[256,256]{1,0:T(8,128)(2,1)S(1)}, u32[]{:S(2)}, u32[]{:S(2)}) collective-permute-start(bf16[256,256]{1,0:T(8,128)(2,1)S(1)} %collective-permute-done), channel_id=1, source_target_pairs={{0,8},{8,16},{16,24},{24,32},{32,40},{40,48},{48,56},{56,64},{64,7... | collective-permute-start | bytes 393224 | tf_op jit(solution)/shard_map/ppermute | solution.py:19
  52.0 4.4 collective-permute-start.3
  58.9 2.4 copy-start.3
  58.9 2.4 copy-start.4
  58.9 2.5 copy-start.5
  61.3 1.9 copy-start.6
  63.1 0.9 copy-start.2
  83.6 127.3 %collective-permute-start.4 = (f32[2,128,256]{2,1,0:T(8,128)}, f32[2,128,256]{2,1,0:T(8,128)}, u32[]{:S(2)}, u32[]{:S(2)}) collective-permute-start(f32[2,128,256]{2,1,0:T(8,128)} %get-tuple-element.33), channel_id=1, source_target_pairs={{0,1},{1,2},{2,3},{3,4},{4,5},{5,6},{6,7},{7,0},{8,9},{9,10},{10,1... | collective-permute-start | bytes 786440 | tf_op jit(solution)/shard_map/ppermute | solution.py:13
  92.3 122.4 %collective-permute-start.6 = (f32[2,128,256]{2,1,0:T(8,128)}, f32[2,128,256]{2,1,0:T(8,128)S(1)}, u32[]{:S(2)}, u32[]{:S(2)}) collective-permute-start(f32[2,128,256]{2,1,0:T(8,128)} %get-tuple-element.32), channel_id=1, source_target_pairs={{0,7},{1,0},{2,1},{3,2},{4,3},{5,4},{6,5},{7,6},{8,15},{9,8},{10,9... | collective-permute-start | bytes 786440 | tf_op jit(solution)/shard_map/ppermute | solution.py:13
  210.9 355.1 %collective-permute-start.5 = (f32[2,128,256]{2,1,0:T(8,128)}, f32[2,128,256]{2,1,0:T(8,128)}, u32[]{:S(2)}, u32[]{:S(2)}) collective-permute-start(f32[2,128,256]{2,1,0:T(8,128)} %collective-permute-done.4), channel_id=1, source_target_pairs={{0,8},{8,16},{16,24},{24,32},{32,40},{40,48},{48,56},{56,64},{64,7... | collective-permute-start | bytes 786440 | tf_op jit(solution)/shard_map/ppermute | solution.py:19
  214.7 353.0 %collective-permute-start.7 = (f32[2,128,256]{2,1,0:T(8,128)S(1)}, f32[2,128,256]{2,1,0:T(8,128)}, u32[]{:S(2)}, u32[]{:S(2)}) collective-permute-start(f32[2,128,256]{2,1,0:T(8,128)S(1)} %collective-permute-done.6), channel_id=1, source_target_pairs={{8,0},{16,8},{24,16},{32,24},{40,32},{48,40},{56,48},{64,56},{72,6... | collective-permute-start | bytes 786440 | tf_op jit(solution)/shard_map/ppermute | solution.py:19
Sparse Core Ops, SparseCore 0:
  102.9 461.4 all-reduce.1
where the time goes:
time: 579 us
  waiting for transfers between devices  361 us (62%)
  blocking collectives  108 us (19%)
  starting transfers between devices  53.7 us (9%)
  other arithmetic  18.4 us (3%)
  between operations  14.3 us (2%)
  local copies, waits for them, and re-layouts  13.2 us (2%)
  matrix products  10.2 us (2%)
    psum x1, waiting for transfers between devices, on_device(): lax.psum((partial_weight, partial_bias), ('rows', 'cols'))  338 us
    psum x1, blocking collectives, on_device(): lax.psum((partial_weight, partial_bias), ('rows', 'cols'))  108 us
    ppermute x4, starting transfers between devices, shifted(): return lax.ppermute(value, axis, pairs)  36.7 us
    ppermute x4, waiting for transfers between devices, shifted(): return lax.ppermute(value, axis, pairs)  19.8 us
    ppermute x4, starting transfers between devices, from_behind(): lax.ppermute(value, axis, [(source, source + steps) for source in range(i...  16.9 us
  transfers between devices with their start and end apart: 9, of which 4 were waited for; matrix products, arithmetic and copies ran while one was open for 2% of the time, Pallas kernels for 0%

commit v1 on v0

--- a/solution.py
+++ b/solution.py
@@ -73,7 +73,7 @@
         aggregated, grad_pre, (((0,), (0,)), ((), ())), preferred_element_type=jnp.float32
     )
     partial_bias = jnp.sum(grad_pre.astype(jnp.float32), axis=0)
-    total_weight, total_bias = lax.psum((partial_weight, partial_bias), ("rows", "cols"))
+    total_weight, total_bias = lax.psum(lax.psum((partial_weight, partial_bias), "cols"), "rows")
     nodes_total = features.shape[0] * lax.axis_size("rows") * lax.axis_size("cols")
     norm_scale = 1.0 / math.sqrt(nodes_total)
     grad_weight = total_weight * norm_scale

time: 579 us -> 1180 us (2.04)
  the two profiles are of different devices: /device:TPU:4 before, /device:TPU:8 now
where the time goes in v1:
time: 1180 us
  waiting for transfers between devices  835 us (71%)
  blocking collectives  247 us (21%)
  starting transfers between devices  39.3 us (3%)
  other arithmetic  18.4 us (2%)
  between operations  14.3 us (1%)
  local copies, waits for them, and re-layouts  13.1 us (1%)
    psum x1, waiting for transfers between devices, on_device(): lax.psum(lax.psum((partial_weight, partial_bias), 'cols'), 'rows')  773 us
    psum x1, blocking collectives, on_device(): lax.psum(lax.psum((partial_weight, partial_bias), 'cols'), 'rows')  212 us
    ppermute x4, waiting for transfers between devices, shifted(): return lax.ppermute(value, axis, pairs)  61 us
    psum x1, blocking collectives, on_device(): lax.psum((partial_weight, partial_bias), 'cols')  35.4 us
    ppermute x4, starting transfers between devices, shifted(): return lax.ppermute(value, axis, pairs)  33.1 us
  transfers between devices with their start and end apart: 10, of which 5 were waited for; matrix products, arithmetic and copies ran while one was open for 1% of the time, Pallas kernels for 0%

profile of v1, /device:TPU:8, one launch (start us, length us, event | category | flops | bytes accessed | tf_op | source)
XLA Modules:
  0.0 1178.1 jit_solution(7441362721036428152)
XLA Ops:
  8.4 15.7 %collective-permute-start = (bf16[256,256]{1,0:T(8,128)(2,1)S(1)}, bf16[256,256]{1,0:T(8,128)(2,1)S(1)}, u32[]{:S(2)}, u32[]{:S(2)}) collective-permute-start(bf16[256,256]{1,0:T(8,128)(2,1)S(1)} %get-tuple-element.35), channel_id=1, source_target_pairs={{0,1},{1,2},{2,3},{3,4},{4,5},{5,6},{6,7},{7,0},{8,9},{9,10},{10,1... | collective-permute-start | bytes 393224 | tf_op jit(solution)/shard_map/ppermute | solution.py:13
  24.1 1.9 collective-permute-start.2
  27.6 9.6 collective-permute-done
  38.8 13.7 %collective-permute-done.2 = bf16[256,256]{1,0:T(8,128)(2,1)S(1)} collective-permute-done((bf16[256,256]{1,0:T(8,128)(2,1)S(1)}, bf16[256,256]{1,0:T(8,128)(2,1)S(1)}, u32[]{:S(2)}, u32[]{:S(2)}) %collective-permute-start.2) | collective-permute-done | bytes 131104 | tf_op jit(solution)/shard_map/ppermute | solution.py:13
  53.9 1.9 collective-permute-done.3
  55.9 2.3 gather_fusion
  58.2 2.4 bitcast_convert_fusion
  60.6 1.8 convert_reduce_fusion
  63.7 3.1 broadcast_select_fusion
  66.8 6.1 copy.17
  73.1 8.9 scatter_fusion
  82.8 8.1 collective-permute-start.4
  90.9 7.3 collective-permute-start.6
  98.3 2.5 fusion.12
  100.8 37.6 %collective-permute-done.4 = f32[2,128,256]{2,1,0:T(8,128)} collective-permute-done((f32[2,128,256]{2,1,0:T(8,128)}, f32[2,128,256]{2,1,0:T(8,128)}, u32[]{:S(2)}, u32[]{:S(2)}) %collective-permute-start.4) | collective-permute-done | bytes 262176 | tf_op jit(solution)/shard_map/ppermute | solution.py:13
  138.4 2.2 collective-permute-start.5
  140.7 35.4 %psum.30 = f32[256]{0:T(256)S(1)} all-reduce(f32[256]{0:T(256)S(1)} %get-tuple-element.28), channel_id=1, replica_groups=mesh['rows'=64,'cols'=8] {'cols'}, use_global_device_ids=true, to_apply=%region_4.5 | all-reduce | flops 256 | bytes 2048 | tf_op jit(solution)/shard_map/psum | solution.py:76
  176.1 212.0 %psum.31 = f32[256]{0:T(256)S(1)} all-reduce(f32[256]{0:T(256)S(1)} %psum.30), channel_id=1, replica_groups=mesh['rows'=64,'cols'=8] {'rows'}, use_global_device_ids=true, to_apply=%region_5.6 | all-reduce | flops 256 | bytes 2048 | tf_op jit(solution)/shard_map/psum | solution.py:76
  389.9 1.3 slice.73
  391.3 1.7 fusion.7
  393.0 1.7 fusion.6
  394.7 2.4 convert_element_type.37
  397.1 772.5 %all-reduce.5.cloned.1.call-done = f32[256,256]{1,0:T(8,128)} async-done(((f32[256,256]{1,0:T(8,128)}), f32[256,256]{1,0:T(8,128)}) %all-reduce.5.cloned.1.call-update) | async-done | bytes 262160 | tf_op jit(solution)/shard_map/psum | solution.py:76
  1169.6 1.7 broadcast_multiply_fusion
  (43 shorter events, 9.9 us)
Async XLA Ops:
  7.2 51.0 %copy-start = (bf16[12,3,128,128]{3,2,1,0:T(8,128)(2,1)S(1)}, bf16[12,3,128,128]{3,2,1,0:T(8,128)(2,1)}, u32[]{:S(2)}) copy-start(bf16[12,3,128,128]{3,2,1,0:T(8,128)(2,1)} %param.12) | copy-start | bytes 3538948
  7.2 48.6 %copy-start.1 = (bf16[1536,256]{1,0:T(8,128)(2,1)S(1)}, bf16[1536,256]{1,0:T(8,128)(2,1)}, u32[]{:S(2)}) copy-start(bf16[1536,256]{1,0:T(8,128)(2,1)} %param.11) | copy-start | bytes 2359300
  7.2 384.1 %all-reduce.3.cloned.1.call-start = ((), (), s32[]{:S(2)}) async-start(), calls=%async_computation | async-start | bytes 524288 | tf_op jit(solution)/shard_map/psum | solution.py:76
  8.4 28.9 %collective-permute-start = (bf16[256,256]{1,0:T(8,128)(2,1)S(1)}, bf16[256,256]{1,0:T(8,128)(2,1)S(1)}, u32[]{:S(2)}, u32[]{:S(2)}) collective-permute-start(bf16[256,256]{1,0:T(8,128)(2,1)S(1)} %get-tuple-element.35), channel_id=1, source_target_pairs={{0,1},{1,2},{2,3},{3,4},{4,5},{5,6},{6,7},{7,0},{8,9},{9,10},{10,1... | collective-permute-start | bytes 393224 | tf_op jit(solution)/shard_map/ppermute | solution.py:13
  24.1 28.4 %collective-permute-start.2 = (bf16[256,256]{1,0:T(8,128)(2,1)S(1)}, bf16[256,256]{1,0:T(8,128)(2,1)S(1)}, u32[]{:S(2)}, u32[]{:S(2)}) collective-permute-start(bf16[256,256]{1,0:T(8,128)(2,1)S(1)} %get-tuple-element.36), channel_id=1, source_target_pairs={{0,7},{1,0},{2,1},{3,2},{4,3},{5,4},{6,5},{7,6},{8,15},{9,8},{10,9... | collective-permute-start | bytes 393224 | tf_op jit(solution)/shard_map/ppermute | solution.py:13
  37.3 16.5 %collective-permute-start.1 = (bf16[256,256]{1,0:T(8,128)(2,1)S(1)}, bf16[256,256]{1,0:T(8,128)(2,1)S(1)}, u32[]{:S(2)}, u32[]{:S(2)}) collective-permute-start(bf16[256,256]{1,0:T(8,128)(2,1)S(1)} %collective-permute-done), channel_id=1, source_target_pairs={{0,8},{8,16},{16,24},{24,32},{32,40},{40,48},{48,56},{56,64},{64,7... | collective-permute-start | bytes 393224 | tf_op jit(solution)/shard_map/ppermute | solution.py:19
  52.5 3.2 collective-permute-start.3
  58.2 2.4 copy-start.3
  58.2 2.4 copy-start.4
  58.2 2.5 copy-start.5
  60.6 1.9 copy-start.6
  62.4 0.9 copy-start.2
  82.8 55.6 %collective-permute-start.4 = (f32[2,128,256]{2,1,0:T(8,128)}, f32[2,128,256]{2,1,0:T(8,128)}, u32[]{:S(2)}, u32[]{:S(2)}) collective-permute-start(f32[2,128,256]{2,1,0:T(8,128)} %get-tuple-element.33), channel_id=1, source_target_pairs={{0,1},{1,2},{2,3},{3,4},{4,5},{5,6},{6,7},{7,0},{8,9},{9,10},{10,1... | collective-permute-start | bytes 786440 | tf_op jit(solution)/shard_map/ppermute | solution.py:13
  90.9 297.2 %collective-permute-start.6 = (f32[2,128,256]{2,1,0:T(8,128)}, f32[2,128,256]{2,1,0:T(8,128)S(1)}, u32[]{:S(2)}, u32[]{:S(2)}) collective-permute-start(f32[2,128,256]{2,1,0:T(8,128)} %get-tuple-element.32), channel_id=1, source_target_pairs={{0,7},{1,0},{2,1},{3,2},{4,3},{5,4},{6,5},{7,6},{8,15},{9,8},{10,9... | collective-permute-start | bytes 786440 | tf_op jit(solution)/shard_map/ppermute | solution.py:13
  100.8 1068.8 %all-reduce.5.cloned.1.call-start = ((), (), s32[]{:S(2)}) async-start(), calls=%async_computation.1 | async-start | bytes 524288 | tf_op jit(solution)/shard_map/psum | solution.py:76
  138.4 252.9 %collective-permute-start.5 = (f32[2,128,256]{2,1,0:T(8,128)}, f32[2,128,256]{2,1,0:T(8,128)}, u32[]{:S(2)}, u32[]{:S(2)}) collective-permute-start(f32[2,128,256]{2,1,0:T(8,128)} %collective-permute-done.4), channel_id=1, source_target_pairs={{0,8},{8,16},{16,24},{24,32},{32,40},{40,48},{48,56},{56,64},{64,7... | collective-permute-start | bytes 786440 | tf_op jit(solution)/shard_map/ppermute | solution.py:19
  388.1 4.9 collective-permute-start.7
Sparse Core Ops, SparseCore 0:
  100.9 171.8 all-reduce.2
  391.4 778.1 all-reduce.4
